TPU v7x, 32 devices: a whole 2x2x4 slice. The times are simulated.
32 devices in a mesh: blk: 8 (over z, x), rep: 4 (over y, core).
Axes of the slice: x: 2, y: 2, z: 4, core: 2. Of those that a mesh axis runs over, the one named last changes fastest.
Arguments:
- points: bfloat16 [6144, 1024], P('blk'), may hold values from -6 to 6
- w_in: bfloat16 [1024, 512], replicated, may hold values from -0.1875 to 0.1875
- b_in: float32 [512], replicated, may hold values from -3 to 3
- w_out: bfloat16 [512, 64], replicated, may hold values from -0.25 to 0.25
- inv_scale: float32 [64], replicated, may hold values from 0.05 to 0.5
- solves: bfloat16 [64, 6144], P(None, 'blk'), may hold values from -1.6875 to 1.6875
- probes: bfloat16 [64, 6144], P(None, 'blk'), may hold values from -1.6875 to 1.6875
Outputs:
- feat_grad: float32 [64, 6144], P(None, ('blk', 'rep'))
- grad_w_in: float32 [1024, 512], replicated
- grad_b_in: float32 [512], replicated
- grad_w_out: float32 [512, 64], replicated
All inputs are finite; a program needn't handle non-finite values.
Results may differ from a plain program's by a relative error of at most 0.034.
Values may be sent and summed in bfloat16 or wider, within the bound.
No kernel may reach another device: no remote copies, remote signals or barrier semaphores. Data moves between devices by JAX's collectives and lax.ppermute only.
A program may use at most 64 MiB of HBM per device.

v0:
```python
import math
import jax
import jax.numpy as jnp
from jax import lax
from jax.sharding import PartitionSpec as P


def shifted(block, axis, distance):
    devices = range(lax.axis_size(axis))
    route = [((i - distance) % len(devices), i) for i in devices]
    return lax.ppermute(block, axis, route)


def couple(own_y, own_pair, own_sq, visitor, feat):
    vis_y = visitor[:feat]
    vis_pair = visitor[feat:]
    vis_sq = jnp.sum(jnp.square(vis_y.astype(jnp.float32)), axis=0)
    cross = lax.dot_general(
        own_y, vis_y, (((0,), (0,)), ((), ())), preferred_element_type=jnp.float32
    )
    kernel = jnp.exp(-0.5 * (own_sq[:, None] + vis_sq[None, :] - 2.0 * cross))
    coupling = lax.dot_general(
        own_pair, vis_pair, (((0,), (0,)), ((), ())), preferred_element_type=jnp.float32
    )
    weight_b = (coupling * kernel).astype(jnp.bfloat16)
    totals = jnp.sum(weight_b.astype(jnp.float32), axis=1)
    pull = lax.dot_general(
        vis_y, weight_b, (((1,), (1,)), ((), ())), preferred_element_type=jnp.float32
    )
    return (totals, pull)


def on_device(points, w_in, b_in, w_out, inv_scale, solves, probes):
    feat = w_out.shape[1]
    reps = lax.axis_size("rep")
    blocks = lax.axis_size("blk")
    rep_index = lax.axis_index("rep")
    rows = points.shape[0]
    quarter = rows // reps
    first = rep_index * quarter
    npts = rows * blocks
    levels = reps.bit_length() - 1
    own_points = lax.dynamic_slice_in_dim(points, first, quarter, 0)
    hidden = jnp.tanh(jnp.dot(points, w_in, preferred_element_type=jnp.float32) + b_in).astype(
        jnp.bfloat16
    )
    pre = lax.dot_general(
        w_out, hidden, (((0,), (1,)), ((), ())), preferred_element_type=jnp.float32
    )
    hidden, scaled = (hidden, (pre * inv_scale[:, None]).astype(jnp.bfloat16))
    own_hidden = lax.dynamic_slice_in_dim(hidden, first, quarter, 0)
    own_pair = jnp.concatenate([solves, probes], axis=0)
    own_sq = jnp.sum(jnp.square(scaled.astype(jnp.float32)), axis=0)
    scaled32 = scaled.astype(jnp.float32)
    visitor = jnp.concatenate([scaled, probes, solves], axis=0)
    for bit in range(levels):
        moved = shifted(visitor, "blk", -(1 << bit))
        visitor = jnp.where(rep_index // (1 << bit) % 2 == 1, moved, visitor)

    def accumulate(state, vis):
        totals, pull = couple(scaled, own_pair, own_sq, vis, feat)
        return (state[0] + totals, state[1] + pull)

    init = (jnp.zeros((rows,), jnp.float32), jnp.zeros((feat, rows), jnp.float32))
    steps = blocks // reps

    def advance(index, carry):
        state, vis = carry
        state = accumulate(state, vis)
        return (state, shifted(vis, "blk", -reps))

    state, last_vis = lax.fori_loop(0, steps - 1, advance, (init, visitor))
    state = accumulate(state, last_vis)
    totals, pull = state
    drift = pull - scaled32 * totals[None, :]
    summed = lax.psum_scatter(drift, "rep", scatter_dimension=1, tiled=True)
    feat_grad = summed * inv_scale[:, None]
    grad_b16 = feat_grad.astype(jnp.bfloat16)
    back = lax.dot_general(
        grad_b16, w_out, (((0,), (1,)), ((), ())), preferred_element_type=jnp.float32
    )
    hid32 = own_hidden.astype(jnp.float32)
    pre_grad = back * (1.0 - hid32 * hid32)
    norm = 1.0 / math.sqrt(npts)
    term_w_in = (
        lax.dot_general(
            own_points,
            pre_grad.astype(jnp.bfloat16),
            (((0,), (0,)), ((), ())),
            preferred_element_type=jnp.float32,
        )
        * norm
    )
    term_b_in = jnp.sum(pre_grad, axis=0) * norm
    term_w_out = (
        lax.dot_general(
            own_hidden, grad_b16, (((0,), (1,)), ((), ())), preferred_element_type=jnp.float32
        )
        * norm
    )
    grad_w_in, grad_b_in, grad_w_out = lax.psum((term_w_in, term_b_in, term_w_out), ("blk", "rep"))
    return (feat_grad, grad_w_in, grad_b_in, grad_w_out)


def solution(mesh):
    in_specs = (P("blk", None), P(), P(), P(), P(), P(None, "blk"), P(None, "blk"))
    out_specs = (P(None, ("blk", "rep")), P(), P(), P())
    return jax.shard_map(
        on_device, mesh=mesh, in_specs=in_specs, out_specs=out_specs, check_vma=False
    )
```

profile of v0, /device:TPU:0, one launch (start us, length us, event | category | flops | bytes accessed | tf_op | source)
XLA Modules:
  0.0 224.5 jit_solution(10279714449616067677)
XLA Ops:
  7.3 1.3 copy-done
  8.6 2.2 tanh_convert_fusion
  10.8 0.4 fusion.3
  11.2 6.1 %collective-permute-start = (bf16[192,768]{1,0:T(8,128)(2,1)S(1)}, bf16[192,768]{1,0:T(8,128)(2,1)S(1)}, u32[]{:S(2)}, u32[]{:S(2)}) collective-permute-start(bf16[192,768]{1,0:T(8,128)(2,1)S(1)} %pad_maximum_fusion), channel_id=1, source_target_pairs={{4,0},{8,4},{12,8},{16,12},{20,16},{24,20},{28,24},{0,28},{5,1},{9... | collective-permute-start | bytes 884744 | tf_op jit(solution)/shard_map/ppermute | solution.py:11
  17.3 6.3 %collective-permute-done = bf16[192,768]{1,0:T(8,128)(2,1)S(1)} collective-permute-done((bf16[192,768]{1,0:T(8,128)(2,1)S(1)}, bf16[192,768]{1,0:T(8,128)(2,1)S(1)}, u32[]{:S(2)}, u32[]{:S(2)}) %collective-permute-start) | collective-permute-done | bytes 294944 | tf_op jit(solution)/shard_map/ppermute | solution.py:11
  23.6 1.6 collective-permute-start.1
  25.3 6.3 %collective-permute-done.1 = bf16[192,768]{1,0:T(8,128)(2,1)S(1)} collective-permute-done((bf16[192,768]{1,0:T(8,128)(2,1)S(1)}, bf16[192,768]{1,0:T(8,128)(2,1)S(1)}, u32[]{:S(2)}, u32[]{:S(2)}) %collective-permute-start.1) | collective-permute-done | bytes 294944 | tf_op jit(solution)/shard_map/ppermute | solution.py:11
  31.6 0.6 collective-permute-start.2
  32.3 0.5 fusion.13
  32.8 0.9 convert_reduce_fusion.1
  33.7 12.2 %collective-permute-done.2 = bf16[192,768]{1,0:T(8,128)(2,1)S(1)} collective-permute-done((bf16[192,768]{1,0:T(8,128)(2,1)S(1)}, bf16[192,768]{1,0:T(8,128)(2,1)S(1)}, u32[]{:S(2)}, u32[]{:S(2)}) %collective-permute-start.2) | collective-permute-done | bytes 294944 | tf_op jit(solution)/shard_map/while/body/eval_jaxpr/ppermute | solution.py:11
  46.0 0.5 fusion.10
  46.5 0.9 convert_reduce_fusion
  47.4 0.3 fusion.8
  47.8 0.3 fusion
  48.1 0.9 copy.11
  49.1 22.9 %reduce-scatter.4.cloned.1.call-done = f32[192,64]{1,0:T(8,128)} async-done(((f32[768,64]{1,0:T(8,128)}), f32[192,64]{1,0:T(8,128)}) %reduce-scatter.4.cloned.1.call-update) | async-done | bytes 49168
  72.0 1.0 copy.12
  73.3 0.8 convolution_multiply_fusion.3
  74.1 1.8 convolution_multiply_fusion
  76.0 39.6 %psum.22 = f32[512]{0:T(512)} all-reduce(f32[512]{0:T(512)S(1)} %broadcast_multiply_fusion.1), channel_id=1, replica_groups=mesh['blk'=8,'rep'=4] {'blk','rep'}, use_global_device_ids=true, to_apply=%region_8.9 | all-reduce | flops 512 | bytes 4096 | tf_op jit(solution)/shard_map/psum | solution.py:101
  115.6 98.3 %all-reduce.3.cloned.1.call-done = (f32[1024,512]{1,0:T(8,128)}, f32[512,64]{0,1:T(8,128)}) async-done(((f32[1024,512]{1,0:T(8,128)}, f32[512,64]{0,1:T(8,128)}), (f32[1024,512]{1,0:T(8,128)}, f32[512,64]{0,1:T(8,128)})) %all-reduce.3.cloned.1.call-update) | async-done | bytes 2228240 | tf_op jit(solution)/shard_map/psum | solution.py:101
  213.9 3.1 %copy.16 = f32[1024,512]{1,0:T(8,128)} copy(f32[1024,512]{1,0:T(8,128)} %get-tuple-element.38) | data formatting | bytes 4194304
  217.0 0.7 copy.17
  (28 shorter events, 0.7 us)
Async XLA Ops:
  7.2 1.4 copy-start
  7.2 3.6 %copy-start.6 = (f32[64]{0:T(128)S(1)}, f32[64]{0:T(128)}, u32[]{:S(2)}) copy-start(f32[64]{0:T(128)} %param.11) | copy-start | bytes 772
  7.2 3.6 %copy-start.5 = (bf16[512,64]{0,1:T(8,128)(2,1)S(1)}, bf16[512,64]{0,1:T(8,128)(2,1)}, u32[]{:S(2)}) copy-start(bf16[512,64]{0,1:T(8,128)(2,1)} %param.10) | copy-start | bytes 196612
  7.2 4.0 %copy-start.1 = (bf16[64,768]{1,0:T(8,128)(2,1)S(1)}, bf16[64,768]{1,0:T(8,128)(2,1)}, u32[]{:S(2)}) copy-start(bf16[64,768]{1,0:T(8,128)(2,1)} %param.12) | copy-start | bytes 294916
  7.2 4.0 %copy-start.2 = (bf16[64,768]{1,0:T(8,128)(2,1)S(1)}, bf16[64,768]{1,0:T(8,128)(2,1)}, u32[]{:S(2)}) copy-start(bf16[64,768]{1,0:T(8,128)(2,1)} %param.13) | copy-start | bytes 294916
  7.2 64.8 %reduce-scatter.4.cloned.1.call-start = ((), (), s32[]{:S(2)}) async-start(), calls=%async_computation.1 | async-start | bytes 491520
  11.2 12.3 %collective-permute-start = (bf16[192,768]{1,0:T(8,128)(2,1)S(1)}, bf16[192,768]{1,0:T(8,128)(2,1)S(1)}, u32[]{:S(2)}, u32[]{:S(2)}) collective-permute-start(bf16[192,768]{1,0:T(8,128)(2,1)S(1)} %pad_maximum_fusion), channel_id=1, source_target_pairs={{4,0},{8,4},{12,8},{16,12},{20,16},{24,20},{28,24},{0,28},{5,1},{9... | collective-permute-start | bytes 884744 | tf_op jit(solution)/shard_map/ppermute | solution.py:11
  23.6 7.9 %collective-permute-start.1 = (bf16[192,768]{1,0:T(8,128)(2,1)S(1)}, bf16[192,768]{1,0:T(8,128)(2,1)S(1)}, u32[]{:S(2)}, u32[]{:S(2)}) collective-permute-start(bf16[192,768]{1,0:T(8,128)(2,1)S(1)} %broadcast_select_fusion), channel_id=1, source_target_pairs={{8,0},{12,4},{16,8},{20,12},{24,16},{28,20},{0,24},{4,28},{9,1},{1... | collective-permute-start | bytes 884744 | tf_op jit(solution)/shard_map/ppermute | solution.py:11
  31.6 14.3 %collective-permute-start.2 = (bf16[192,768]{1,0:T(8,128)(2,1)S(1)}, bf16[192,768]{1,0:T(8,128)(2,1)S(1)}, u32[]{:S(2)}, u32[]{:S(2)}) collective-permute-start(bf16[192,768]{1,0:T(8,128)(2,1)S(1)} %broadcast_select_fusion.1), channel_id=1, source_target_pairs={{16,0},{20,4},{24,8},{28,12},{0,16},{4,20},{8,24},{12,28},{17,1},{... | collective-permute-start | bytes 884744 | tf_op jit(solution)/shard_map/while/body/eval_jaxpr/ppermute | solution.py:11
  49.1 164.8 %all-reduce.3.cloned.1.call-start = ((), (), s32[]{:S(2)}) async-start(), calls=%async_computation.2 | async-start | bytes 4456448 | tf_op jit(solution)/shard_map/psum | solution.py:101
  73.0 2.9 %copy-start.3 = (f32[64,192]{1,0:T(8,128)}, f32[64,192]{1,0:T(8,128)S(1)}, u32[]{:S(2)}) copy-start(f32[64,192]{1,0:T(8,128)S(1)} %broadcast_multiply_fusion) | copy-start | bytes 147460
  213.9 3.1 %copy-start.4 = (f32[512,64]{0,1:T(8,128)S(1)}, f32[512,64]{0,1:T(8,128)}, u32[]{:S(2)}) copy-start(f32[512,64]{0,1:T(8,128)} %get-tuple-element.40) | copy-start | bytes 393220
Sparse Core Ops, SparseCore 0:
  49.2 22.7 reduce-scatter.3
  78.1 135.7 all-reduce.2
where the time goes:
time: 225 us; the launch traced here: 224 us
  waiting for transfers between devices  146 us (65%)
  blocking collectives  39.6 us (18%)
  between operations  14.2 us (6%)
  matrix products  8.95 us (4%)
  starting transfers between devices  8.36 us (4%)
  local copies, waits for them, and re-layouts  7.02 us (3%)
    psum x1, waiting for transfers between devices, on_device(): lax.psum((term_w_in, term_b_in, term_w_out), ('blk', 'rep'))  98.3 us
    psum x1, blocking collectives, on_device(): lax.psum((term_w_in, term_b_in, term_w_out), ('blk', 'rep'))  39.6 us
    ppermute x3, waiting for transfers between devices, shifted(): return lax.ppermute(block, axis, route)  24.8 us
    unnamed x3, waiting for transfers between devices  22.9 us
    ppermute x3, starting transfers between devices, shifted(): return lax.ppermute(block, axis, route)  8.29 us
    unnamed x19, local copies, waits for them, and re-layouts  7.01 us
  transfers between devices with their start and end apart: 5, of which 5 were waited for; matrix products, arithmetic and copies ran while one was open for 1% of the time, Pallas kernels for 0%

commit v1 on v0

--- a/solution.py
+++ b/solution.py
@@ -98,7 +98,9 @@
         )
         * norm
     )
-    grad_w_in, grad_b_in, grad_w_out = lax.psum((term_w_in, term_b_in, term_w_out), ("blk", "rep"))
+    grad_w_in, grad_b_in, grad_w_out = lax.psum(
+        lax.psum((term_w_in, term_b_in, term_w_out), "blk"), "rep"
+    )
     return (feat_grad, grad_w_in, grad_b_in, grad_w_out)
 
 

time: 225 us -> 248 us (1.10)
  waiting for transfers between devices: 146 us -> 183 us
  blocking collectives: 39.6 us -> 26.5 us
    psum x1 -> x2, waiting for transfers between devices: 98.3 us -> 135 us  [the longest x1 106 us: on_device(): lax.psum((term_w_in, term_b_in, term_w_out), 'blk')]
    psum x1 -> x2, blocking collectives: 39.6 us -> 26.5 us  [the longest x1 19.4 us: on_device(): lax.psum((term_w_in, term_b_in, term_w_out), 'blk')]
    unnamed x3 -> x4, waiting for transfers between devices: 22.9 us -> 22.9 us
  transfers between devices with their start and end apart: 5 -> 6, of which waited for: 5 -> 6; matrix products, arithmetic and copies ran while one was open for 1% -> 1% of each run, Pallas kernels for 0% -> 0%
where the time goes in v1:
time: 248 us
  waiting for transfers between devices  183 us (74%)
  blocking collectives  26.5 us (11%)
  between operations  13.9 us (6%)
  matrix products  8.95 us (4%)
  starting transfers between devices  8.41 us (3%)
  local copies, waits for them, and re-layouts  7.02 us (3%)
    psum x1, waiting for transfers between devices, on_device(): lax.psum((term_w_in, term_b_in, term_w_out), 'blk')  106 us
    psum x1, waiting for transfers between devices, on_device(): lax.psum(lax.psum((term_w_in, term_b_in, term_w_out), 'blk'), 'rep')  28.9 us
    ppermute x3, waiting for transfers between devices, shifted(): return lax.ppermute(block, axis, route)  24.8 us
    unnamed x4, waiting for transfers between devices  22.9 us
    psum x1, blocking collectives, on_device(): lax.psum((term_w_in, term_b_in, term_w_out), 'blk')  19.4 us
    ppermute x3, starting transfers between devices, shifted(): return lax.ppermute(block, axis, route)  8.29 us
    psum x1, blocking collectives, on_device(): lax.psum(lax.psum((term_w_in, term_b_in, term_w_out), 'blk'), 'rep')  7.03 us
    unnamed x19, local copies, waits for them, and re-layouts  7.01 us
  transfers between devices with their start and end apart: 6, of which 6 were waited for; matrix products, arithmetic and copies ran while one was open for 1% of the time, Pallas kernels for 0%

profile of v1, /device:TPU:0, one launch (start us, length us, event | category | flops | bytes accessed | tf_op | source)
XLA Modules:
  0.0 247.8 jit_solution(8985244965857009644)
XLA Ops:
  7.3 1.3 copy-done
  8.6 2.2 tanh_convert_fusion
  10.8 0.4 fusion.3
  11.2 6.1 %collective-permute-start = (bf16[192,768]{1,0:T(8,128)(2,1)S(1)}, bf16[192,768]{1,0:T(8,128)(2,1)S(1)}, u32[]{:S(2)}, u32[]{:S(2)}) collective-permute-start(bf16[192,768]{1,0:T(8,128)(2,1)S(1)} %pad_maximum_fusion), channel_id=1, source_target_pairs={{4,0},{8,4},{12,8},{16,12},{20,16},{24,20},{28,24},{0,28},{5,1},{9... | collective-permute-start | bytes 884744 | tf_op jit(solution)/shard_map/ppermute | solution.py:11
  17.3 6.3 %collective-permute-done = bf16[192,768]{1,0:T(8,128)(2,1)S(1)} collective-permute-done((bf16[192,768]{1,0:T(8,128)(2,1)S(1)}, bf16[192,768]{1,0:T(8,128)(2,1)S(1)}, u32[]{:S(2)}, u32[]{:S(2)}) %collective-permute-start) | collective-permute-done | bytes 294944 | tf_op jit(solution)/shard_map/ppermute | solution.py:11
  23.6 1.6 collective-permute-start.1
  25.3 6.3 %collective-permute-done.1 = bf16[192,768]{1,0:T(8,128)(2,1)S(1)} collective-permute-done((bf16[192,768]{1,0:T(8,128)(2,1)S(1)}, bf16[192,768]{1,0:T(8,128)(2,1)S(1)}, u32[]{:S(2)}, u32[]{:S(2)}) %collective-permute-start.1) | collective-permute-done | bytes 294944 | tf_op jit(solution)/shard_map/ppermute | solution.py:11
  31.6 0.6 collective-permute-start.2
  32.3 0.5 fusion.13
  32.8 0.9 convert_reduce_fusion.1
  33.7 12.2 %collective-permute-done.2 = bf16[192,768]{1,0:T(8,128)(2,1)S(1)} collective-permute-done((bf16[192,768]{1,0:T(8,128)(2,1)S(1)}, bf16[192,768]{1,0:T(8,128)(2,1)S(1)}, u32[]{:S(2)}, u32[]{:S(2)}) %collective-permute-start.2) | collective-permute-done | bytes 294944 | tf_op jit(solution)/shard_map/while/body/eval_jaxpr/ppermute | solution.py:11
  46.0 0.5 fusion.10
  46.5 0.9 convert_reduce_fusion
  48.1 0.9 copy.11
  49.1 22.9 %reduce-scatter.4.cloned.1.call-done = f32[192,64]{1,0:T(8,128)} async-done(((f32[768,64]{1,0:T(8,128)}), f32[192,64]{1,0:T(8,128)}) %reduce-scatter.4.cloned.1.call-update) | async-done | bytes 49168
  72.0 1.0 copy.12
  73.3 0.8 convolution_multiply_fusion.3
  74.1 1.8 convolution_multiply_fusion
  76.0 106.1 %all-reduce.5.cloned.1.call-done = (f32[1024,512]{1,0:T(8,128)}, f32[512,64]{0,1:T(8,128)}) async-done(((f32[1024,512]{1,0:T(8,128)}, f32[512,64]{0,1:T(8,128)}), (f32[1024,512]{1,0:T(8,128)}, f32[512,64]{0,1:T(8,128)})) %all-reduce.5.cloned.1.call-update) | async-done | bytes 2228240 | tf_op jit(solution)/shard_map/psum | solution.py:102
  182.1 19.4 %psum.44 = f32[512]{0:T(512)S(1)} all-reduce(f32[512]{0:T(512)S(1)} %broadcast_multiply_fusion.1), channel_id=1, replica_groups=mesh['blk'=8,'rep'=4] {'blk'}, use_global_device_ids=true, to_apply=%region_9.10 | all-reduce | flops 512 | bytes 4096 | tf_op jit(solution)/shard_map/psum | solution.py:102
  201.6 7.0 %psum.45 = f32[512]{0:T(512)} all-reduce(f32[512]{0:T(512)S(1)} %psum.44), channel_id=1, replica_groups=mesh['blk'=8,'rep'=4] {'rep'}, use_global_device_ids=true, to_apply=%region_10.11 | all-reduce | flops 512 | bytes 4096 | tf_op jit(solution)/shard_map/psum | solution.py:101
  208.6 28.9 %all-reduce.7.cloned.1.call-done = (f32[1024,512]{1,0:T(8,128)}, f32[512,64]{0,1:T(8,128)}) async-done(((f32[1024,512]{1,0:T(8,128)}, f32[512,64]{0,1:T(8,128)}), (f32[1024,512]{1,0:T(8,128)}, f32[512,64]{0,1:T(8,128)})) %all-reduce.7.cloned.1.call-update) | async-done | bytes 2228240 | tf_op jit(solution)/shard_map/psum | solution.py:101
  237.5 3.1 %copy.18 = f32[1024,512]{1,0:T(8,128)} copy(f32[1024,512]{1,0:T(8,128)} %get-tuple-element.40) | data formatting | bytes 4194304
  240.6 0.7 copy.19
  (32 shorter events, 1.4 us)
Async XLA Ops:
  7.2 1.4 copy-start
  7.2 3.6 %copy-start.6 = (f32[64]{0:T(128)S(1)}, f32[64]{0:T(128)}, u32[]{:S(2)}) copy-start(f32[64]{0:T(128)} %param.11) | copy-start | bytes 772
  7.2 3.6 %copy-start.5 = (bf16[512,64]{0,1:T(8,128)(2,1)S(1)}, bf16[512,64]{0,1:T(8,128)(2,1)}, u32[]{:S(2)}) copy-start(bf16[512,64]{0,1:T(8,128)(2,1)} %param.10) | copy-start | bytes 196612
  7.2 4.0 %copy-start.1 = (bf16[64,768]{1,0:T(8,128)(2,1)S(1)}, bf16[64,768]{1,0:T(8,128)(2,1)}, u32[]{:S(2)}) copy-start(bf16[64,768]{1,0:T(8,128)(2,1)} %param.12) | copy-start | bytes 294916
  7.2 4.0 %copy-start.2 = (bf16[64,768]{1,0:T(8,128)(2,1)S(1)}, bf16[64,768]{1,0:T(8,128)(2,1)}, u32[]{:S(2)}) copy-start(bf16[64,768]{1,0:T(8,128)(2,1)} %param.13) | copy-start | bytes 294916
  7.2 64.8 %reduce-scatter.4.cloned.1.call-start = ((), (), s32[]{:S(2)}) async-start(), calls=%async_computation.1 | async-start | bytes 491520
  11.2 12.3 %collective-permute-start = (bf16[192,768]{1,0:T(8,128)(2,1)S(1)}, bf16[192,768]{1,0:T(8,128)(2,1)S(1)}, u32[]{:S(2)}, u32[]{:S(2)}) collective-permute-start(bf16[192,768]{1,0:T(8,128)(2,1)S(1)} %pad_maximum_fusion), channel_id=1, source_target_pairs={{4,0},{8,4},{12,8},{16,12},{20,16},{24,20},{28,24},{0,28},{5,1},{9... | collective-permute-start | bytes 884744 | tf_op jit(solution)/shard_map/ppermute | solution.py:11
  23.6 7.9 %collective-permute-start.1 = (bf16[192,768]{1,0:T(8,128)(2,1)S(1)}, bf16[192,768]{1,0:T(8,128)(2,1)S(1)}, u32[]{:S(2)}, u32[]{:S(2)}) collective-permute-start(bf16[192,768]{1,0:T(8,128)(2,1)S(1)} %broadcast_select_fusion), channel_id=1, source_target_pairs={{8,0},{12,4},{16,8},{20,12},{24,16},{28,20},{0,24},{4,28},{9,1},{1... | collective-permute-start | bytes 884744 | tf_op jit(solution)/shard_map/ppermute | solution.py:11
  31.6 14.3 %collective-permute-start.2 = (bf16[192,768]{1,0:T(8,128)(2,1)S(1)}, bf16[192,768]{1,0:T(8,128)(2,1)S(1)}, u32[]{:S(2)}, u32[]{:S(2)}) collective-permute-start(bf16[192,768]{1,0:T(8,128)(2,1)S(1)} %broadcast_select_fusion.1), channel_id=1, source_target_pairs={{16,0},{20,4},{24,8},{28,12},{0,16},{4,20},{8,24},{12,28},{17,1},{... | collective-permute-start | bytes 884744 | tf_op jit(solution)/shard_map/while/body/eval_jaxpr/ppermute | solution.py:11
  49.1 133.0 %all-reduce.5.cloned.1.call-start = ((), (), s32[]{:S(2)}) async-start(), calls=%async_computation.2 | async-start | bytes 4456448 | tf_op jit(solution)/shard_map/psum | solution.py:102
  73.0 2.9 %copy-start.3 = (f32[64,192]{1,0:T(8,128)}, f32[64,192]{1,0:T(8,128)S(1)}, u32[]{:S(2)}) copy-start(f32[64,192]{1,0:T(8,128)S(1)} %broadcast_multiply_fusion) | copy-start | bytes 147460
  75.9 161.6 %all-reduce.7.cloned.1.call-start = ((), (), s32[]{:S(2)}) async-start(), calls=%async_computation.3 | async-start | bytes 4456448 | tf_op jit(solution)/shard_map/psum | solution.py:101
  237.5 3.1 %copy-start.4 = (f32[512,64]{0,1:T(8,128)S(1)}, f32[512,64]{0,1:T(8,128)}, u32[]{:S(2)}) copy-start(f32[512,64]{0,1:T(8,128)} %get-tuple-element.42) | copy-start | bytes 393220
Sparse Core Ops, SparseCore 0:
  49.2 22.7 reduce-scatter.3
  76.2 105.8 all-reduce.4
  184.6 52.8 all-reduce.6
